TPU v7x, 512 devices: a whole 4x4x16 slice. The times are simulated.
512 devices in a mesh: bl: 32 (over y, x, core), dir: 16 (over z).
Axes of the slice: x: 4, y: 4, z: 16, core: 2. Of those that a mesh axis runs over, the one named last changes fastest.
Arguments:
- visibilities: float32 [8, 16, 8192], P(None, 'dir', 'bl'), may hold values from -24 to 24
- coherencies: bfloat16 [32, 8, 16, 8192], P('dir', None, None, 'bl'), may hold values from -6 to 6
- gain_offsets: float32 [32, 8, 512], P(None, None, 'bl'), may hold values from -1.5 to 1.5
- stations: int32 [2, 8192], P(None, 'bl'), may hold values from 0 to 511, as said below
- solve_order: int32 [32], replicated, may hold values from 0 to 31, each once
- counts: int32 [32], replicated, may hold values from 1 to 2
- damping: int32 [32], replicated, may hold values from 1 to 8
Outputs:
- gains: float32 [32, 8, 512], P(None, None, 'bl')
- residual: float32 [8, 16, 8192], P(None, 'dir', 'bl')
Inputs may be any that keep to these rules, and one draw needn't show every extreme that they name: Each baseline names two different stations. `solve_order`: each direction appears once.
All inputs are finite; a program needn't handle non-finite values.
Results may differ from a plain program's by a relative error of at most 0.0003.
Values may be sent and summed in bfloat16 or wider, within the bound.
A program may use at most 64 MiB of HBM per device.

v0:
```python
import jax
import jax.numpy as jnp
from jax import lax
from jax.sharding import PartitionSpec as P

LM_ITERS = 2
SOLVED = 4


def matrix_entry(mat, i, j):
    return (mat[4 * i + 2 * j], mat[4 * i + 2 * j + 1])


def matmul_two(left, right):
    pieces = []
    for i in (0, 1):
        for j in (0, 1):
            left_r0, left_i0 = matrix_entry(left, i, 0)
            left_r1, left_i1 = matrix_entry(left, i, 1)
            right_r0, right_i0 = matrix_entry(right, 0, j)
            right_r1, right_i1 = matrix_entry(right, 1, j)
            pieces.append(
                left_r0 * right_r0 - left_i0 * right_i0 + left_r1 * right_r1 - left_i1 * right_i1
            )
            pieces.append(
                left_r0 * right_i0 + left_i0 * right_r0 + left_r1 * right_i1 + left_i1 * right_r1
            )
    return jnp.stack(pieces)


def adjoint(mat):
    return jnp.stack([mat[0], -mat[1], mat[4], -mat[5], mat[2], -mat[3], mat[6], -mat[7]])


def apply_gains(gain_p, coher_now, gain_q):
    return matmul_two(matmul_two(gain_p, coher_now), adjoint(gain_q))


def gram_parts(gram):
    return jnp.stack([gram[0], gram[6], gram[2], gram[3]])


def station_terms(gain_p, gain_q, coher_now, target):
    z_rows = matmul_two(coher_now, adjoint(gain_q))
    y_rows = matmul_two(adjoint(coher_now), adjoint(gain_p))
    leading_endpoint = jnp.concatenate(
        [matmul_two(target, adjoint(z_rows)), gram_parts(matmul_two(z_rows, adjoint(z_rows)))], 0
    )
    second = jnp.concatenate(
        [
            matmul_two(adjoint(target), adjoint(y_rows)),
            gram_parts(matmul_two(y_rows, adjoint(y_rows))),
        ],
        0,
    )
    return (jnp.sum(leading_endpoint, axis=1), jnp.sum(second, axis=1))


def solve_station(gathered_sums, gain_now, damp_value):
    numerator = gathered_sums[:8] + damp_value * gain_now
    diag_a = gathered_sums[8] + damp_value
    diag_d = gathered_sums[9] + damp_value
    cross_r = gathered_sums[10]
    cross_i = gathered_sums[11]
    determinant = diag_a * diag_d - cross_r * cross_r - cross_i * cross_i
    zeros_row = jnp.zeros_like(determinant)
    inverse = (
        jnp.stack([diag_d, zeros_row, -cross_r, -cross_i, -cross_r, cross_i, diag_a, zeros_row])
        / determinant
    )
    return matmul_two(numerator, inverse)


def on_device(visibilities, coherencies, gain_offsets, stations, solve_order, counts, damping):
    identity = jnp.zeros((8,), jnp.float32).at[0].set(1.0).at[6].set(1.0)
    start = lax.all_gather(gain_offsets, "bl", axis=2, tiled=True) + identity[None, :, None]
    groups = lax.axis_size("bl")
    total_channels = coherencies.shape[2]
    station_count = start.shape[2]
    damping_factor = visibilities.shape[2] * groups * total_channels / station_count
    coher_all = lax.all_to_all(coherencies, "dir", 2, 0, tiled=True)
    ends_p = jnp.take(start, stations[0], axis=2)
    ends_q = jnp.take(start, stations[1], axis=2)
    gain_p = jnp.transpose(ends_p, (1, 0, 2))[:, :, None, :]
    gain_q = jnp.transpose(ends_q, (1, 0, 2))[:, :, None, :]
    coher_f32 = jnp.transpose(coher_all, (1, 0, 2, 3)).astype(jnp.float32)
    first_model = jnp.sum(apply_gains(gain_p, coher_f32, gain_q), axis=1)
    first_residual = visibilities - first_model

    def direction_model(gain_now, coher_now):
        gain_p = jnp.take(gain_now, stations[0], axis=1)[:, None, :]
        gain_q = jnp.take(gain_now, stations[1], axis=1)[:, None, :]
        return apply_gains(gain_p, coher_now, gain_q)

    def sweep(step_index, state):
        gain_table, residual = state
        which = solve_order[step_index]
        coher_now = lax.dynamic_index_in_dim(coher_all, which, 0, keepdims=False).astype(
            jnp.float32
        )
        damp_value = damping[which].astype(jnp.float32) * damping_factor
        gain_start = gain_table[which]
        target = residual + direction_model(gain_start, coher_now)

        def iterate(round_index, gain_now):
            gain_p = jnp.take(gain_now, stations[0], axis=1)[:, None, :]
            gain_q = jnp.take(gain_now, stations[1], axis=1)[:, None, :]
            leading_endpoint, second = station_terms(gain_p, gain_q, coher_now, target)
            local_sums = (
                jax.ops.segment_sum(leading_endpoint.T, stations[0], station_count)
                + jax.ops.segment_sum(second.T, stations[1], station_count)
            ).T
            gathered_sums = lax.psum(local_sums, ("bl", "dir"))
            return solve_station(gathered_sums, gain_now, damp_value)

        rounds = jnp.clip(counts[which], 0, LM_ITERS)
        gain_final = lax.fori_loop(0, rounds, iterate, gain_start)
        residual = target - direction_model(gain_final, coher_now)
        return (gain_table.at[which].set(gain_final), residual)

    gain_table, residual = lax.fori_loop(0, SOLVED, sweep, (start, first_residual))
    own_width = station_count // groups
    gains = lax.dynamic_slice_in_dim(gain_table, lax.axis_index("bl") * own_width, own_width, 2)
    return (gains, residual)


def solution(mesh):
    return jax.shard_map(
        on_device,
        mesh=mesh,
        in_specs=(
            P(None, "dir", "bl"),
            P("dir", None, None, "bl"),
            P(None, None, "bl"),
            P(None, "bl"),
            P(),
            P(),
            P(),
        ),
        out_specs=(P(None, None, "bl"), P(None, "dir", "bl")),
        check_vma=False,
    )
```

profile of v0, /device:TPU:1, one launch (start us, length us, event | category | flops | bytes accessed | tf_op | source)
XLA Modules:
  0.0 847.1 jit_solution(9811879134477437065)
XLA Ops:
  0.6 1.6 copy.1122
  2.2 15.7 %all-to-all-start = ((bf16[2,8,16,256]{3,1,0,2:T(8,128)(2,1)}), bf16[2,8,16,256]{3,1,0,2:T(8,128)(2,1)S(1)}, u32[]{:S(2)}, u32[]{:S(2)}) async-start(bf16[2,8,16,256]{3,1,0,2:T(8,128)(2,1)} %copy.1122), calls=%async_computation | async-start | bytes 262144 | tf_op jit(solution)/shard_map/all_to_all | solution.py:81
  18.0 0.8 fusion.135
  18.8 0.9 copy.1120
  19.7 27.2 %all_gather.3 = f32[32,8,512]{0,1,2:T(8,128)S(1)} all-gather(f32[32,8,16]{0,1,2:T(8,128)S(1)} %copy.1120), channel_id=1, replica_groups=mesh['bl'=32,'dir'=16] {'bl'}, dimensions={2}, use_global_device_ids=true | all-gather | bytes 540672 | tf_op jit(solution)/shard_map/all_gather | solution.py:76
  47.1 0.9 copy.1133
  48.0 2.0 gather_fusion.7
  50.0 1.6 copy.1124
  51.6 2.0 gather_fusion.6
  53.6 1.6 copy.1121
  57.4 788.4 %while.42 = (s32[]{:T(128)}, f32[32,8,512]{2,1,0:T(8,128)S(1)}, f32[8,1,256]{2,1,0:T(1,128)S(1)}, s32[32]{0:T(128)S(1)}, s32[32]{0:T(128)S(1)}, /*index=5*/bf16[...) while((s32[]{:T(128)}, f32[32,8,512]{2,1,0:T(8,128)S(1)}, ...), condition=%wide.region_8.12_spmd, body=%wide.region_1.11_spmd.sunk | while | flops 253464 | bytes 1958014 | solution.py:121
  60.3 0.7 gather_fusion.2
  64.8 109.2 %while.43 = (s32[]{:T(128)}, f32[8,512]{1,0:T(8,128)S(1)}, s32[]{:T(128)}, s32[2,256]{1,0:T(2,128)S(1)}, f32[8,1,256]{2,1,0:T(1,128)S(1)}, /*index=5*/f32[8,1,25...) while((s32[]{:T(128)}, f32[8,512]{1,0:T(8,128)S(1)}, ...), condition=%wide.region_7.10_spmd, body=%wide.region_3.9_spmd.sunk | while | flops 160768 | bytes 1263793 | solution.py:117
  65.0 0.7 gather_fusion
  66.0 0.7 gather_fusion.1
  67.0 1.5 scatter_custom_fusion.11
  69.0 1.5 scatter_custom_fusion.10
  70.6 103.1 %psum.9 = f32[12,512]{1,0:T(8,128)S(1)} all-reduce(f32[12,512]{1,0:T(8,128)S(1)} %add_bitcast_fusion.2), channel_id=1, replica_groups=mesh['bl'=32,'dir'=16] {'bl','dir'}, use_global_device_ids=true, to_apply=%region_6.8 | all-reduce | flops 6144 | bytes 49152 | tf_op jit(solution)/shard_map/while/body/eval_jaxpr/while/body/psum | solution.py:113
  174.1 0.7 gather_fusion.4
  174.9 0.7 gather_fusion.5
  175.9 0.8 and_reduce_fusion.2
  184.6 212.3 %while.43 = (s32[]{:T(128)}, f32[8,512]{1,0:T(8,128)S(1)}, s32[]{:T(128)}, s32[2,256]{1,0:T(2,128)S(1)}, f32[8,1,256]{2,1,0:T(1,128)S(1)}, /*index=5*/f32[8,1,25...) while((s32[]{:T(128)}, f32[8,512]{1,0:T(8,128)S(1)}, ...), condition=%wide.region_7.10_spmd, body=%wide.region_3.9_spmd.sunk | while | flops 160768 | bytes 1263793 | solution.py:117
  184.8 0.7 gather_fusion
  185.8 0.7 gather_fusion.1
  186.8 1.5 scatter_custom_fusion.11
  188.8 1.5 scatter_custom_fusion.10
  190.4 100.7 %psum.9 = f32[12,512]{1,0:T(8,128)S(1)} all-reduce(f32[12,512]{1,0:T(8,128)S(1)} %add_bitcast_fusion.2), channel_id=1, replica_groups=mesh['bl'=32,'dir'=16] {'bl','dir'}, use_global_device_ids=true, to_apply=%region_6.8 | all-reduce | flops 6144 | bytes 49152 | tf_op jit(solution)/shard_map/while/body/eval_jaxpr/while/body/psum | solution.py:113
  291.6 0.7 gather_fusion
  292.5 0.7 gather_fusion.1
  293.6 1.5 scatter_custom_fusion.11
  295.5 1.5 scatter_custom_fusion.10
  297.2 99.4 %psum.9 = f32[12,512]{1,0:T(8,128)S(1)} all-reduce(f32[12,512]{1,0:T(8,128)S(1)} %add_bitcast_fusion.2), channel_id=1, replica_groups=mesh['bl'=32,'dir'=16] {'bl','dir'}, use_global_device_ids=true, to_apply=%region_6.8 | all-reduce | flops 6144 | bytes 49152 | tf_op jit(solution)/shard_map/while/body/eval_jaxpr/while/body/psum | solution.py:113
  397.0 0.7 gather_fusion.4
  397.8 0.7 gather_fusion.5
  398.8 0.8 and_reduce_fusion.2
  403.1 0.7 gather_fusion.2
  407.5 212.1 %while.43 = (s32[]{:T(128)}, f32[8,512]{1,0:T(8,128)S(1)}, s32[]{:T(128)}, s32[2,256]{1,0:T(2,128)S(1)}, f32[8,1,256]{2,1,0:T(1,128)S(1)}, /*index=5*/f32[8,1,25...) while((s32[]{:T(128)}, f32[8,512]{1,0:T(8,128)S(1)}, ...), condition=%wide.region_7.10_spmd, body=%wide.region_3.9_spmd.sunk | while | flops 160768 | bytes 1263793 | solution.py:117
  407.7 0.7 gather_fusion
  408.7 0.7 gather_fusion.1
  409.7 1.5 scatter_custom_fusion.11
  411.7 1.5 scatter_custom_fusion.10
  413.3 100.4 %psum.9 = f32[12,512]{1,0:T(8,128)S(1)} all-reduce(f32[12,512]{1,0:T(8,128)S(1)} %add_bitcast_fusion.2), channel_id=1, replica_groups=mesh['bl'=32,'dir'=16] {'bl','dir'}, use_global_device_ids=true, to_apply=%region_6.8 | all-reduce | flops 6144 | bytes 49152 | tf_op jit(solution)/shard_map/while/body/eval_jaxpr/while/body/psum | solution.py:113
  514.1 0.7 gather_fusion
  515.1 0.7 gather_fusion.1
  516.2 1.5 scatter_custom_fusion.11
  518.1 1.5 scatter_custom_fusion.10
  519.7 99.6 %psum.9 = f32[12,512]{1,0:T(8,128)S(1)} all-reduce(f32[12,512]{1,0:T(8,128)S(1)} %add_bitcast_fusion.2), channel_id=1, replica_groups=mesh['bl'=32,'dir'=16] {'bl','dir'}, use_global_device_ids=true, to_apply=%region_6.8 | all-reduce | flops 6144 | bytes 49152 | tf_op jit(solution)/shard_map/while/body/eval_jaxpr/while/body/psum | solution.py:113
  619.7 0.7 gather_fusion.4
  620.5 0.7 gather_fusion.5
  621.5 0.8 and_reduce_fusion.2
  630.2 212.2 %while.43 = (s32[]{:T(128)}, f32[8,512]{1,0:T(8,128)S(1)}, s32[]{:T(128)}, s32[2,256]{1,0:T(2,128)S(1)}, f32[8,1,256]{2,1,0:T(1,128)S(1)}, /*index=5*/f32[8,1,25...) while((s32[]{:T(128)}, f32[8,512]{1,0:T(8,128)S(1)}, ...), condition=%wide.region_7.10_spmd, body=%wide.region_3.9_spmd.sunk | while | flops 160768 | bytes 1263793 | solution.py:117
  630.4 0.7 gather_fusion
  631.4 0.7 gather_fusion.1
  632.5 1.5 scatter_custom_fusion.11
  634.4 1.5 scatter_custom_fusion.10
  636.0 100.5 %psum.9 = f32[12,512]{1,0:T(8,128)S(1)} all-reduce(f32[12,512]{1,0:T(8,128)S(1)} %add_bitcast_fusion.2), channel_id=1, replica_groups=mesh['bl'=32,'dir'=16] {'bl','dir'}, use_global_device_ids=true, to_apply=%region_6.8 | all-reduce | flops 6144 | bytes 49152 | tf_op jit(solution)/shard_map/while/body/eval_jaxpr/while/body/psum | solution.py:113
  737.0 0.7 gather_fusion
  737.9 0.7 gather_fusion.1
  739.0 1.5 scatter_custom_fusion.11
  740.9 1.5 scatter_custom_fusion.10
  742.5 99.6 %psum.9 = f32[12,512]{1,0:T(8,128)S(1)} all-reduce(f32[12,512]{1,0:T(8,128)S(1)} %add_bitcast_fusion.2), channel_id=1, replica_groups=mesh['bl'=32,'dir'=16] {'bl','dir'}, use_global_device_ids=true, to_apply=%region_6.8 | all-reduce | flops 6144 | bytes 49152 | tf_op jit(solution)/shard_map/while/body/eval_jaxpr/while/body/psum | solution.py:113
  842.5 0.7 gather_fusion.4
  843.3 0.7 gather_fusion.5
  844.3 0.8 and_reduce_fusion.2
  (563 shorter events, 31.6 us)
Async XLA Ops:
  0.6 46.2 %copy-start.4 = (f32[8]{0:T(128)S(1)}, f32[8]{0:T(128)}, u32[]{:S(2)}) copy-start(f32[8]{0:T(128)} %constant.188.clone.1) | copy-start | bytes 100
  2.2 53.1 %all-to-all-start = ((bf16[2,8,16,256]{3,1,0,2:T(8,128)(2,1)}), bf16[2,8,16,256]{3,1,0,2:T(8,128)(2,1)S(1)}, u32[]{:S(2)}, u32[]{:S(2)}) async-start(bf16[2,8,16,256]{3,1,0,2:T(8,128)(2,1)} %copy.1122), calls=%async_computation | async-start | bytes 262144 | tf_op jit(solution)/shard_map/all_to_all | solution.py:81
  55.2 2.1 copy-start.3
  55.2 2.1 copy-start
  55.3 2.1 copy-start.2
  55.3 2.1 copy-start.5
  55.3 2.1 copy-start.6
  55.3 2.1 copy-start.7
  845.8 1.3 copy-start.1
where the time goes:
time: 849 us; the launch traced here: 847 us
  blocking collectives  731 us (86%)
  local copies, waits for them, and re-layouts  49.5 us (6%)
  other arithmetic  35.1 us (4%)
  starting transfers between devices  15.7 us (2%)
  loops' own time  15.3 us (2%)
    psum x7, blocking collectives, iterate(): gathered_sums = lax.psum(local_sums, ('bl', 'dir'))  703 us
    all_gather x1, blocking collectives, on_device(): lax.all_gather(gain_offsets, 'bl', axis=2, tiled=True)  27.2 us
  transfers between devices with their start and end apart: 1, of which 0 were waited for; matrix products, arithmetic and copies ran while one was open for 1% of the time, Pallas kernels for 0%

commit v1 on v0

--- a/solution.py
+++ b/solution.py
@@ -110,7 +110,7 @@
                 jax.ops.segment_sum(leading_endpoint.T, stations[0], station_count)
                 + jax.ops.segment_sum(second.T, stations[1], station_count)
             ).T
-            gathered_sums = lax.psum(local_sums, ("bl", "dir"))
+            gathered_sums = jnp.sum(lax.all_gather(local_sums, ("bl", "dir")), axis=0)
             return solve_station(gathered_sums, gain_now, damp_value)
 
         rounds = jnp.clip(counts[which], 0, LM_ITERS)

time: 849 us -> 1720 us (2.03)
  waiting for transfers between devices: 0.01 us -> 1510 us
  blocking collectives: 731 us -> 27.2 us
  other arithmetic: 35.1 us -> 82 us
    all_gather x0 -> x7, waiting for transfers between devices: none -> 1510 us  [iterate(): gathered_sums = jnp.sum(lax.all_gather(local_sums, ('bl', 'dir')), axis=0)]
    psum x7 -> x0, blocking collectives: 703 us -> none  [iterate(): gathered_sums = lax.psum(local_sums, ('bl', 'dir'))]
    reduce_sum x0 -> x7, other arithmetic: none -> 47.2 us  [iterate(): gathered_sums = jnp.sum(lax.all_gather(local_sums, ('bl', 'dir')), axis=0)]
  transfers between devices with their start and end apart: 1 -> 8, of which waited for: 0 -> 7; matrix products, arithmetic and copies ran while one was open for 1% -> 1% of each run, Pallas kernels for 0% -> 0%
where the time goes in v1:
time: 1720 us
  waiting for transfers between devices  1510 us (88%)
  other arithmetic  82 us (5%)
  local copies, waits for them, and re-layouts  52.7 us (3%)
  blocking collectives  27.2 us (2%)
    all_gather x7, waiting for transfers between devices, iterate(): gathered_sums = jnp.sum(lax.all_gather(local_sums, ('bl', 'dir')), axis=0)  1510 us
    reduce_sum x7, other arithmetic, iterate(): gathered_sums = jnp.sum(lax.all_gather(local_sums, ('bl', 'dir')), axis=0)  47.2 us
  transfers between devices with their start and end apart: 8, of which 7 were waited for; matrix products, arithmetic and copies ran while one was open for 1% of the time, Pallas kernels for 0%

profile of v1, /device:TPU:1, one launch (start us, length us, event | category | flops | bytes accessed | tf_op | source)
XLA Modules:
  0.0 1719.9 jit_solution(1394755886773002978)
XLA Ops:
  7.2 1.6 copy.697
  8.8 15.7 all-to-all-start
  24.5 0.8 fusion.135
  25.3 0.9 copy.695
  26.2 27.2 %all_gather.11 = f32[32,8,512]{0,1,2:T(8,128)S(1)} all-gather(f32[32,8,16]{0,1,2:T(8,128)S(1)} %copy.695), channel_id=1, replica_groups=mesh['bl'=32,'dir'=16] {'bl'}, dimensions={2}, use_global_device_ids=true | all-gather | bytes 540672 | tf_op jit(solution)/shard_map/all_gather | solution.py:76
  53.6 0.9 copy.708
  54.5 2.0 gather_fusion.7
  56.6 1.6 copy.699
  58.1 2.0 gather_fusion.6
  60.2 1.6 copy.696
  64.0 1647.8 %while.42 = (s32[]{:T(128)}, f32[32,8,512]{2,1,0:T(8,128)S(1)}, f32[8,1,256]{2,1,0:T(1,128)S(1)}, s32[32]{0:T(128)S(1)}, s32[32]{0:T(128)S(1)}, /*index=5*/bf16[...) while((s32[]{:T(128)}, f32[32,8,512]{2,1,0:T(8,128)S(1)}, ...), condition=%wide.region_8.12_spmd, body=%wide.region_1.11_spmd.sunk | while | flops 3386904 | bytes 56492200 | solution.py:121
  71.3 232.4 %while.43 = (s32[]{:T(128)}, f32[8,512]{1,0:T(8,128)S(1)}, s32[]{:T(128)}, s32[2,256]{1,0:T(2,128)S(1)}, f32[8,1,256]{2,1,0:T(1,128)S(1)}, /*index=5*/f32[8,1,25...) while((s32[]{:T(128)}, f32[8,512]{1,0:T(8,128)S(1)}, ...), condition=%wide.region_7.10_spmd, body=%wide.region_3.9_spmd.sunk | while | flops 3294208 | bytes 55797980 | solution.py:117
  71.6 0.7 gather_fusion
  73.9 1.5 scatter_custom_fusion.11
  75.4 1.5 scatter_custom_fusion.10
  76.9 0.7 copy.753
  77.7 219.0 %all-gather.6.cloned.1.call-done = f32[512,12,512]{2,1,0:T(8,128)} async-done(((f32[1,12,512]{2,1,0:T(8,128)}), f32[512,12,512]{2,1,0:T(8,128)}) %all-gather.6.cloned.1.call-update) | async-done | bytes 12582928 | tf_op jit(solution)/shard_map/while/body/eval_jaxpr/while/body/all_gather | solution.py:113
  296.7 6.7 reduce_sum.37
  303.8 0.7 gather_fusion.4
  304.6 0.7 gather_fusion.5
  314.1 457.8 %while.43 = (s32[]{:T(128)}, f32[8,512]{1,0:T(8,128)S(1)}, s32[]{:T(128)}, s32[2,256]{1,0:T(2,128)S(1)}, f32[8,1,256]{2,1,0:T(1,128)S(1)}, /*index=5*/f32[8,1,25...) while((s32[]{:T(128)}, f32[8,512]{1,0:T(8,128)S(1)}, ...), condition=%wide.region_7.10_spmd, body=%wide.region_3.9_spmd.sunk | while | flops 3294208 | bytes 55797980 | solution.py:117
  314.4 0.7 gather_fusion
  316.7 1.5 scatter_custom_fusion.11
  318.2 1.5 scatter_custom_fusion.10
  319.8 0.7 copy.753
  320.5 215.5 %all-gather.6.cloned.1.call-done = f32[512,12,512]{2,1,0:T(8,128)} async-done(((f32[1,12,512]{2,1,0:T(8,128)}), f32[512,12,512]{2,1,0:T(8,128)}) %all-gather.6.cloned.1.call-update) | async-done | bytes 12582928 | tf_op jit(solution)/shard_map/while/body/eval_jaxpr/while/body/all_gather | solution.py:113
  536.0 6.7 reduce_sum.37
  543.3 0.7 gather_fusion
  545.6 1.5 scatter_custom_fusion.11
  547.1 1.5 scatter_custom_fusion.10
  548.7 0.7 copy.753
  549.4 215.5 %all-gather.6.cloned.1.call-done = f32[512,12,512]{2,1,0:T(8,128)} async-done(((f32[1,12,512]{2,1,0:T(8,128)}), f32[512,12,512]{2,1,0:T(8,128)}) %all-gather.6.cloned.1.call-update) | async-done | bytes 12582928 | tf_op jit(solution)/shard_map/while/body/eval_jaxpr/while/body/all_gather | solution.py:113
  764.9 6.7 reduce_sum.37
  772.1 0.7 gather_fusion.4
  772.9 0.7 gather_fusion.5
  782.4 457.8 %while.43 = (s32[]{:T(128)}, f32[8,512]{1,0:T(8,128)S(1)}, s32[]{:T(128)}, s32[2,256]{1,0:T(2,128)S(1)}, f32[8,1,256]{2,1,0:T(1,128)S(1)}, /*index=5*/f32[8,1,25...) while((s32[]{:T(128)}, f32[8,512]{1,0:T(8,128)S(1)}, ...), condition=%wide.region_7.10_spmd, body=%wide.region_3.9_spmd.sunk | while | flops 3294208 | bytes 55797980 | solution.py:117
  782.7 0.7 gather_fusion
  785.0 1.5 scatter_custom_fusion.11
  786.5 1.5 scatter_custom_fusion.10
  788.0 0.7 copy.753
  788.8 215.5 %all-gather.6.cloned.1.call-done = f32[512,12,512]{2,1,0:T(8,128)} async-done(((f32[1,12,512]{2,1,0:T(8,128)}), f32[512,12,512]{2,1,0:T(8,128)}) %all-gather.6.cloned.1.call-update) | async-done | bytes 12582928 | tf_op jit(solution)/shard_map/while/body/eval_jaxpr/while/body/all_gather | solution.py:113
  1004.3 6.7 reduce_sum.37
  1011.6 0.7 gather_fusion
  1013.9 1.5 scatter_custom_fusion.11
  1015.4 1.5 scatter_custom_fusion.10
  1016.9 0.7 copy.753
  1017.7 215.5 %all-gather.6.cloned.1.call-done = f32[512,12,512]{2,1,0:T(8,128)} async-done(((f32[1,12,512]{2,1,0:T(8,128)}), f32[512,12,512]{2,1,0:T(8,128)}) %all-gather.6.cloned.1.call-update) | async-done | bytes 12582928 | tf_op jit(solution)/shard_map/while/body/eval_jaxpr/while/body/all_gather | solution.py:113
  1233.2 6.7 reduce_sum.37
  1240.3 0.7 gather_fusion.4
  1241.1 0.7 gather_fusion.5
  1250.6 457.8 %while.43 = (s32[]{:T(128)}, f32[8,512]{1,0:T(8,128)S(1)}, s32[]{:T(128)}, s32[2,256]{1,0:T(2,128)S(1)}, f32[8,1,256]{2,1,0:T(1,128)S(1)}, /*index=5*/f32[8,1,25...) while((s32[]{:T(128)}, f32[8,512]{1,0:T(8,128)S(1)}, ...), condition=%wide.region_7.10_spmd, body=%wide.region_3.9_spmd.sunk | while | flops 3294208 | bytes 55797980 | solution.py:117
  1250.9 0.7 gather_fusion
  1253.2 1.5 scatter_custom_fusion.11
  1254.7 1.5 scatter_custom_fusion.10
  1257.0 215.5 %all-gather.6.cloned.1.call-done = f32[512,12,512]{2,1,0:T(8,128)} async-done(((f32[1,12,512]{2,1,0:T(8,128)}), f32[512,12,512]{2,1,0:T(8,128)}) %all-gather.6.cloned.1.call-update) | async-done | bytes 12582928 | tf_op jit(solution)/shard_map/while/body/eval_jaxpr/while/body/all_gather | solution.py:113
  1472.5 6.7 reduce_sum.37
  1479.8 0.7 gather_fusion
  1482.1 1.5 scatter_custom_fusion.11
  1483.6 1.5 scatter_custom_fusion.10
  1485.2 0.7 copy.753
  1485.9 215.5 %all-gather.6.cloned.1.call-done = f32[512,12,512]{2,1,0:T(8,128)} async-done(((f32[1,12,512]{2,1,0:T(8,128)}), f32[512,12,512]{2,1,0:T(8,128)}) %all-gather.6.cloned.1.call-update) | async-done | bytes 12582928 | tf_op jit(solution)/shard_map/while/body/eval_jaxpr/while/body/all_gather | solution.py:113
  1701.4 6.7 reduce_sum.37
  1708.6 0.7 gather_fusion.4
  1709.4 0.7 gather_fusion.5
  (577 shorter events, 40.3 us)
Async XLA Ops:
  7.2 46.2 %copy-start.4 = (f32[8]{0:T(128)S(1)}, f32[8]{0:T(128)}, u32[]{:S(2)}) copy-start(f32[8]{0:T(128)} %constant.188.clone.1) | copy-start | bytes 100
  8.8 53.1 %all-to-all-start = ((bf16[2,8,16,256]{3,1,0,2:T(8,128)(2,1)}), bf16[2,8,16,256]{3,1,0,2:T(8,128)(2,1)S(1)}, u32[]{:S(2)}, u32[]{:S(2)}) async-start(bf16[2,8,16,256]{3,1,0,2:T(8,128)(2,1)} %copy.697), calls=%async_computation | async-start | bytes 262144 | tf_op jit(solution)/shard_map/all_to_all | solution.py:81
  61.8 2.1 copy-start.3
  61.8 2.1 copy-start
  61.8 2.1 copy-start.2
  61.8 2.1 copy-start.5
  61.8 2.1 copy-start.6
  61.8 2.1 copy-start.7
  71.3 225.4 %all-gather.6.cloned.1.call-start = ((), (), s32[]{:S(2)}) async-start(), calls=%async_computation.1 | async-start | bytes 16809984 | tf_op jit(solution)/shard_map/while/body/eval_jaxpr/while/body/all_gather | solution.py:113
  314.1 221.9 %all-gather.6.cloned.1.call-start = ((), (), s32[]{:S(2)}) async-start(), calls=%async_computation.1 | async-start | bytes 16809984 | tf_op jit(solution)/shard_map/while/body/eval_jaxpr/while/body/all_gather | solution.py:113
  543.0 221.9 %all-gather.6.cloned.1.call-start = ((), (), s32[]{:S(2)}) async-start(), calls=%async_computation.1 | async-start | bytes 16809984 | tf_op jit(solution)/shard_map/while/body/eval_jaxpr/while/body/all_gather | solution.py:113
  782.4 221.9 %all-gather.6.cloned.1.call-start = ((), (), s32[]{:S(2)}) async-start(), calls=%async_computation.1 | async-start | bytes 16809984 | tf_op jit(solution)/shard_map/while/body/eval_jaxpr/while/body/all_gather | solution.py:113
  1011.3 221.9 %all-gather.6.cloned.1.call-start = ((), (), s32[]{:S(2)}) async-start(), calls=%async_computation.1 | async-start | bytes 16809984 | tf_op jit(solution)/shard_map/while/body/eval_jaxpr/while/body/all_gather | solution.py:113
  1250.7 221.9 %all-gather.6.cloned.1.call-start = ((), (), s32[]{:S(2)}) async-start(), calls=%async_computation.1 | async-start | bytes 16809984 | tf_op jit(solution)/shard_map/while/body/eval_jaxpr/while/body/all_gather | solution.py:113
  1479.6 221.9 %all-gather.6.cloned.1.call-start = ((), (), s32[]{:S(2)}) async-start(), calls=%async_computation.1 | async-start | bytes 16809984 | tf_op jit(solution)/shard_map/while/body/eval_jaxpr/while/body/all_gather | solution.py:113
  1711.8 1.3 copy-start.1
Sparse Core Ops, SparseCore 0:
  77.8 218.8 all-gather.5
  320.6 215.3 all-gather.5
  549.5 215.3 all-gather.5
  788.9 215.3 all-gather.5
  1017.8 215.3 all-gather.5
  1257.2 215.3 all-gather.5
  1486.1 215.3 all-gather.5
